TPU v7x, 32 devices: a whole 2x2x4 slice. The times are simulated.
32 devices in a mesh: expert: 8 (over z, y), replica: 4 (over x, core).
Axes of the slice: x: 2, y: 2, z: 4, core: 2. Of those that a mesh axis runs over, the one named last changes fastest.
Arguments:
- tokens: bfloat16 [4096, 2048], P(('expert', 'replica')), may hold values from -6 to 6
- out_grad: bfloat16 [4096, 2048], P(('expert', 'replica')), may hold values from -6 to 6
- expert_ids: int32 [4096, 2], P(('expert', 'replica')), may hold values from 0 to 3, as said below
- route_weights: bfloat16 [4096, 2], P(('expert', 'replica')), may hold values from 0.25 to 1
- capacity: int32 [4], replicated, may hold values from 2 to 2
- w_gate: bfloat16 [8, 2048, 384], P('expert', 'replica'), may hold values from -0.125 to 0.125
- w_up: bfloat16 [8, 2048, 384], P('expert', 'replica'), may hold values from -0.125 to 0.125
- w_down: bfloat16 [8, 384, 2048], P('expert', None, 'replica'), may hold values from -0.21875 to 0.21875
Outputs:
- x_grad: bfloat16 [4096, 2048], P(('expert', 'replica'))
- gate_grad: bfloat16 [8, 2048, 384], P('expert', 'replica')
- up_grad: bfloat16 [8, 2048, 384], P('expert', 'replica')
- down_grad: bfloat16 [8, 384, 2048], P('expert')
Inputs may be any that keep to these rules, and one draw needn't show every extreme that they name: `expert_ids`: each row names 2 different experts.
All inputs are finite; a program needn't handle non-finite values.
Results may differ from a plain program's by a relative error of at most 0.009.
Values may be sent and summed in bfloat16 or wider, within the bound.
A program may use at most 64 MiB of HBM per device.

v0:
```python
import jax
import jax.numpy as jnp
from jax import lax
from jax.sharding import PartitionSpec as P

CAP = 2


def shards(tokens, out_grad, expert_ids, route_weights, capacity, w_gate, w_up, w_down):
    experts = capacity.shape[0]
    owners = lax.axis_size("expert")
    width = tokens.shape[1]
    slot_count = experts * CAP
    expert_range = jnp.arange(experts, dtype=jnp.int32)
    chosen = (expert_ids[:, :, None] == expert_range[None, None, :]).astype(jnp.int32)
    ranks = jnp.cumsum(jnp.sum(chosen, axis=1), axis=0)
    place = jnp.sum(chosen * ranks[:, None, :], axis=2) - 1
    limit = jnp.sum(chosen * capacity[None, None, :], axis=2)
    slot_ids = jnp.where(place < limit, expert_ids * CAP + place, -1)
    table = slot_ids[None, :, :] == jnp.arange(slot_count, dtype=jnp.int32)[:, None, None]
    picker = jnp.any(table, axis=2).astype(jnp.bfloat16)
    slot_weight = jnp.sum(
        jnp.where(table, route_weights.astype(jnp.float32)[None, :, :], 0.0), axis=(1, 2)
    ).astype(jnp.bfloat16)
    packed = jnp.dot(
        picker, jnp.concatenate([tokens, out_grad], axis=1), preferred_element_type=jnp.float32
    ).astype(jnp.bfloat16)
    packed = packed.reshape(experts, CAP, 2 * width)
    slot_weight = slot_weight.reshape(experts, CAP)
    send_rows = jnp.broadcast_to(packed[:, None], (experts, 2, CAP, 2 * width)).reshape(
        owners, CAP, 2 * width
    )
    send_weight = jnp.broadcast_to(slot_weight[:, None], (experts, 2, CAP)).reshape(owners, CAP)
    got_rows, got_weight = (
        lax.all_to_all(send_rows, "expert", split_axis=0, concat_axis=0, tiled=True),
        lax.all_to_all(send_weight, "expert", split_axis=0, concat_axis=0, tiled=True),
    )
    gate_all, up_all, down_all = (
        lax.all_gather(w_gate, "replica", axis=1, tiled=True),
        lax.all_gather(w_up, "replica", axis=1, tiled=True),
        lax.all_gather(w_down, "replica", axis=2, tiled=True),
    )
    gate_mat = gate_all[0]
    up_mat = up_all[0]
    down_mat = down_all[0]
    row_total = owners * CAP
    flat_rows = got_rows.reshape(row_total, 2 * width)
    inputs = flat_rows[:, :width]
    cotangent = flat_rows[:, width:]
    weights = got_weight.reshape(row_total).astype(jnp.float32)
    gate = jnp.dot(inputs, gate_mat, preferred_element_type=jnp.float32)
    up = jnp.dot(inputs, up_mat, preferred_element_type=jnp.float32)
    sig = jax.nn.sigmoid(gate)
    act = gate * sig
    hidden = (act * up).astype(jnp.bfloat16)
    scaled = (weights[:, None] * cotangent.astype(jnp.float32)).astype(jnp.bfloat16)
    back = lax.dot_general(
        scaled, down_mat, (((1,), (1,)), ((), ())), preferred_element_type=jnp.float32
    )
    gate_back = (back * up * sig * (1.0 + gate * (1.0 - sig))).astype(jnp.bfloat16)
    up_back = (back * act).astype(jnp.bfloat16)
    both_back = jnp.concatenate([gate_back, up_back], axis=1)
    both_mat = jnp.concatenate([gate_mat, up_mat], axis=1)
    partial_value = lax.dot_general(
        both_back, both_mat, (((1,), (1,)), ((), ())), preferred_element_type=jnp.float32
    ).astype(jnp.bfloat16)
    returned = lax.all_to_all(
        partial_value.reshape(owners, CAP, width), "expert", split_axis=0, concat_axis=0, tiled=True
    )
    returned = returned.reshape(experts, 2, CAP, width)
    total = lax.dot_general(
        picker,
        returned[:, 0].reshape(slot_count, width),
        (((0,), (0,)), ((), ())),
        preferred_element_type=jnp.float32,
    )
    total = total + lax.dot_general(
        picker,
        returned[:, 1].reshape(slot_count, width),
        (((0,), (0,)), ((), ())),
        preferred_element_type=jnp.float32,
    )
    x_grad = total.astype(jnp.bfloat16)
    wide_grad = lax.psum_scatter(
        lax.dot_general(
            inputs, both_back, (((0,), (0,)), ((), ())), preferred_element_type=jnp.float32
        )
        .astype(jnp.bfloat16)
        .astype(jnp.bfloat16),
        "replica",
        scatter_dimension=0,
        tiled=True,
    ).astype(jnp.float32)
    half_units = gate_mat.shape[1]
    gate_grad = wide_grad[:, :half_units].astype(jnp.bfloat16)[None]
    up_grad = wide_grad[:, half_units:].astype(jnp.bfloat16)[None]
    down_local = lax.dot_general(
        hidden, scaled, (((0,), (0,)), ((), ())), preferred_element_type=jnp.float32
    )
    down_grad = lax.psum(down_local.astype(jnp.bfloat16), "replica")[None]
    return (x_grad, gate_grad, up_grad, down_grad)


def solution(mesh):
    return jax.shard_map(
        shards,
        mesh=mesh,
        in_specs=(
            P(("expert", "replica"), None),
            P(("expert", "replica"), None),
            P(("expert", "replica"), None),
            P(("expert", "replica"), None),
            P(),
            P("expert", "replica", None),
            P("expert", "replica", None),
            P("expert", None, "replica"),
        ),
        out_specs=(
            P(("expert", "replica"), None),
            P("expert", "replica", None),
            P("expert", "replica", None),
            P("expert", None, None),
        ),
        check_vma=False,
    )
```

profile of v0, /device:TPU:0, one launch (start us, length us, event | category | flops | bytes accessed | tf_op | source)
XLA Modules:
  0.0 171.9 jit_solution(11029008983379027724)
XLA Ops:
  11.1 0.8 select_reduce_fusion.2
  13.7 7.3 %all-to-all-start = ((bf16[8,1,2]{2,1,0:T(2,128)(2,1)}), bf16[8,1,2]{2,1,0:T(2,128)(2,1)S(1)}, u32[]{:S(2)}, u32[]{:S(2)}) async-start(bf16[8,1,2]{2,1,0:T(2,128)(2,1)} %copy.30), calls=%async_computation | async-start | bytes 8192 | tf_op jit(solution)/shard_map/all_to_all | solution.py:36
  21.0 1.4 convolution_convert_fusion
  22.6 4.9 %all-to-all-done = bf16[8,1,2]{2,1,0:T(2,128)(2,1)S(1)} async-done(((bf16[8,1,2]{2,1,0:T(2,128)(2,1)}), bf16[8,1,2]{2,1,0:T(2,128)(2,1)S(1)}, u32[]{:S(2)}, u32[]{:S(2)}) %all-to-all-start) | async-done | bytes 64 | tf_op jit(solution)/shard_map/all_to_all | solution.py:36
  27.5 0.7 broadcast_in_dim.47
  28.2 3.4 %all-to-all-start.1 = ((bf16[8,2,4096]{2,1,0:T(2,128)(2,1)}), bf16[8,2,4096]{2,1,0:T(2,128)(2,1)S(1)}, u32[]{:S(2)}, u32[]{:S(2)}) async-start(bf16[8,2,4096]{2,1,0:T(2,128)(2,1)} %bitcast), calls=%async_computation.1 | async-start | bytes 262144 | tf_op jit(solution)/shard_map/all_to_all | solution.py:35
  31.7 7.1 %all-to-all-done.1 = bf16[8,2,4096]{2,1,0:T(2,128)(2,1)S(1)} async-done(((bf16[8,2,4096]{2,1,0:T(2,128)(2,1)}), bf16[8,2,4096]{2,1,0:T(2,128)(2,1)S(1)}, u32[]{:S(2)}, u32[]{:S(2)}) %all-to-all-start.1) | async-done | bytes 131104 | tf_op jit(solution)/shard_map/all_to_all | solution.py:35
  38.9 1.8 %fusion.17 = f32[16,384]{1,0:T(8,128)S(1)} fusion(bf16[16,4096]{1,0:T(8,128)(2,1)S(1)} %reshape.48, bf16[1,2048,384]{2,1,0:T(8,128)(2,1)} %all-gather.6.cloned.1.call-done), kind=kOutput, calls=%fused_computation.22 | convolution fusion | flops 25165824 | bytes 1662976 | tf_op jit(solution)/shard_map/dot_general | solution.py:52
  40.7 12.4 %all-gather.4.cloned.1.call-done = bf16[1,384,2048]{2,1,0:T(8,128)(2,1)} async-done(((bf16[1,384,512]{2,1,0:T(8,128)(2,1)}), bf16[1,384,2048]{2,1,0:T(8,128)(2,1)}) %all-gather.4.cloned.1.call-update) | async-done | bytes 1572880 | tf_op jit(solution)/shard_map/all_gather | solution.py:41
  53.1 1.9 %fusion.9 = f32[16,384]{1,0:T(8,128)S(1)} fusion(bf16[1,384,2048]{2,1,0:T(8,128)(2,1)} %all-gather.4.cloned.1.call-done, bf16[16,4096]{1,0:T(8,128)(2,1)S(1)} %reshape.48, f32[16]{0:T(128)S(1)} %reshape.51), kind=kOutput, calls=%fused_computation.11 | convolution fusion | flops 25264128 | bytes 1663488 | tf_op jit(solution)/shard_map/dot_general | solution.py:57
  55.1 19.3 %all-gather.8.cloned.1.call-done = bf16[1,2048,384]{2,1,0:T(8,128)(2,1)} async-done(((bf16[1,512,384]{2,1,0:T(8,128)(2,1)}), bf16[1,2048,384]{2,1,0:T(8,128)(2,1)}) %all-gather.8.cloned.1.call-update) | async-done | bytes 1572880 | tf_op jit(solution)/shard_map/all_gather | solution.py:39
  74.4 1.7 %multiply_convert_fusion.3 = (bf16[16,384]{1,0:T(8,128)(2,1)S(1)}, bf16[16,384]{1,0:T(8,128)(2,1)S(1)}, f32[16,384]{1,0:T(8,128)S(1)}) fusion(f32[16,384]{1,0:T(8,128)S(1)} %fusion.9, f32[16,384]{1,0:T(8,128)S(1)} %fusion.17, bf16[1,2048,384]{2,1,0:T(8,128)(2,1)} %all-gather.8.cloned.1.call-done, bf16[16,4096]{1,0:T(8,128)(2,1)S(1)} %reshape.48), kind=kOutput, calls=%fused_computation.27 | convolution fusion | flops 25245696 | bytes 1736704 | tf_op jit(solution)/shard_map/dot_general | solution.py:51
  76.1 2.7 %convolution_convert_fusion.1 = bf16[2048,768]{1,0:T(8,128)(2,1)} fusion(bf16[16,4096]{1,0:T(8,128)(2,1)S(1)} %reshape.48, bf16[16,384]{1,0:T(8,128)(2,1)S(1)} %get-tuple-element.11, bf16[16,384]{1,0:T(8,128)(2,1)S(1)} %get-tuple-element.10), kind=kOutput, calls=%fused_computation.1 | convolution fusion | flops 51953664 | bytes 3235840 | tf_op jit(solution)/shard_map/dot_general | solution.py:85
  78.8 1.4 copy-done
  80.7 0.9 fusion.6
  81.6 0.7 reshape.49
  82.3 5.5 %all-to-all-start.2 = ((bf16[8,2,2048]{2,1,0:T(2,128)(2,1)}), bf16[8,2,2048]{2,1,0:T(2,128)(2,1)S(1)}, u32[]{:S(2)}, u32[]{:S(2)}) async-start(bf16[8,2,2048]{2,1,0:T(2,128)(2,1)} %reshape.49), calls=%async_computation.2 | async-start | bytes 131072 | tf_op jit(solution)/shard_map/all_to_all | solution.py:67
  87.9 1.8 %fusion.4 = bf16[1,384,2048]{2,1,0:T(8,128)(2,1)} fusion(bf16[16,4096]{1,0:T(8,128)(2,1)S(1)} %reshape.48, f32[16]{0:T(128)S(1)} %reshape.51, f32[16,384]{1,0:T(8,128)S(1)} %fusion.17, f32[16,384]{1,0:T(8,128)S(1)} %get-tuple-element.12), kind=kOutput, calls=%fused_computation.7 | convolution fusion | flops 26087424 | bytes 1688064 | tf_op jit(solution)/shard_map/dot_general | solution.py:97
  89.7 5.1 %all-to-all-done.2 = bf16[8,2,2048]{2,1,0:T(2,128)(2,1)S(1)} async-done(((bf16[8,2,2048]{2,1,0:T(2,128)(2,1)}), bf16[8,2,2048]{2,1,0:T(2,128)(2,1)S(1)}, u32[]{:S(2)}, u32[]{:S(2)}) %all-to-all-start.2) | async-done | bytes 65568 | tf_op jit(solution)/shard_map/all_to_all | solution.py:67
  95.2 1.1 fusion.5
  96.3 20.6 %reduce-scatter.2.cloned.1.call-done = bf16[512,768]{1,0:T(8,128)(2,1)} async-done(((bf16[2048,768]{1,0:T(8,128)(2,1)}), bf16[512,768]{1,0:T(8,128)(2,1)}) %reduce-scatter.2.cloned.1.call-update) | async-done | bytes 786448 | tf_op jit(solution)/shard_map/reduce_scatter | solution.py:84
  116.9 2.1 %slice_bitcast_fusion = (bf16[1,512,384]{2,1,0:T(8,128)(2,1)}, bf16[1,512,384]{2,1,0:T(8,128)(2,1)}) fusion(bf16[512,768]{1,0:T(8,128)(2,1)} %reduce-scatter.2.cloned.1.call-done), kind=kLoop, calls=%fused_computation.16 | loop fusion | bytes 1572864 | tf_op jit(solution)/shard_map/broadcast_in_dim | solution.py:96
  119.0 43.6 %all-reduce.2.cloned.1.call-done = bf16[1,384,2048]{2,1,0:T(8,128)(2,1)} async-done(((bf16[1,384,2048]{2,1,0:T(8,128)(2,1)}), bf16[1,384,2048]{2,1,0:T(8,128)(2,1)}) %all-reduce.2.cloned.1.call-update) | async-done | bytes 1572880 | tf_op jit(solution)/shard_map/psum | solution.py:100
  162.6 2.7 %copy.32 = bf16[1,384,2048]{2,1,0:T(8,128)(2,1)} copy(bf16[1,384,2048]{2,1,0:T(8,128)(2,1)} %all-reduce.2.cloned.1.call-done) | data formatting | bytes 3145728
  (35 shorter events, 7.0 us)
Async XLA Ops:
  7.2 31.8 %all-gather.6.cloned.1.call-start = ((), (), s32[]{:S(2)}) async-start(), calls=%async_computation.5 | async-start | bytes 1966080 | tf_op jit(solution)/shard_map/all_gather | solution.py:40
  7.9 45.2 %all-gather.4.cloned.1.call-start = ((), (), s32[]{:S(2)}) async-start(), calls=%async_computation.4 | async-start | bytes 1966080 | tf_op jit(solution)/shard_map/all_gather | solution.py:41
  8.6 65.7 %all-gather.8.cloned.1.call-start = ((), (), s32[]{:S(2)}) async-start(), calls=%async_computation.6 | async-start | bytes 1966080 | tf_op jit(solution)/shard_map/all_gather | solution.py:39
  13.7 13.7 %all-to-all-start = ((bf16[8,1,2]{2,1,0:T(2,128)(2,1)}), bf16[8,1,2]{2,1,0:T(2,128)(2,1)S(1)}, u32[]{:S(2)}, u32[]{:S(2)}) async-start(bf16[8,1,2]{2,1,0:T(2,128)(2,1)} %copy.30), calls=%async_computation | async-start | bytes 8192 | tf_op jit(solution)/shard_map/all_to_all | solution.py:36
  28.2 10.7 %all-to-all-start.1 = ((bf16[8,2,4096]{2,1,0:T(2,128)(2,1)}), bf16[8,2,4096]{2,1,0:T(2,128)(2,1)S(1)}, u32[]{:S(2)}, u32[]{:S(2)}) async-start(bf16[8,2,4096]{2,1,0:T(2,128)(2,1)} %bitcast), calls=%async_computation.1 | async-start | bytes 262144 | tf_op jit(solution)/shard_map/all_to_all | solution.py:35
  31.6 85.4 %reduce-scatter.2.cloned.1.call-start = ((), (), s32[]{:S(2)}) async-start(), calls=%async_computation.7 | async-start | bytes 3932160 | tf_op jit(solution)/shard_map/reduce_scatter | solution.py:84
  78.8 1.4 copy-start
  78.8 1.9 %copy-start.1 = (bf16[1,2048,384]{2,1,0:T(8,128)(2,1)S(1)}, bf16[1,2048,384]{2,1,0:T(8,128)(2,1)}, u32[]{:S(2)}) copy-start(bf16[1,2048,384]{2,1,0:T(8,128)(2,1)} %all-gather.8.cloned.1.call-done) | copy-start | bytes 4718596
  82.3 12.4 %all-to-all-start.2 = ((bf16[8,2,2048]{2,1,0:T(2,128)(2,1)}), bf16[8,2,2048]{2,1,0:T(2,128)(2,1)S(1)}, u32[]{:S(2)}, u32[]{:S(2)}) async-start(bf16[8,2,2048]{2,1,0:T(2,128)(2,1)} %reshape.49), calls=%async_computation.2 | async-start | bytes 131072 | tf_op jit(solution)/shard_map/all_to_all | solution.py:67
  87.8 74.8 %all-reduce.2.cloned.1.call-start = ((), (), s32[]{:S(2)}) async-start(), calls=%async_computation.8 | async-start | bytes 3145728 | tf_op jit(solution)/shard_map/psum | solution.py:100
Sparse Core Ops, SparseCore 0:
  9.5 22.3 all-gather.5
  33.5 19.6 all-gather.3
  54.7 19.6 all-gather.7
  79.0 37.9 reduce-scatter.1
  119.7 42.8 all-reduce.1
where the time goes:
time: 172 us
  waiting for transfers between devices  115 us (67%)
  starting transfers between devices  16.4 us (10%)
  between operations  13.9 us (8%)
  matrix products  13.7 us (8%)
  local copies, waits for them, and re-layouts  9.59 us (6%)
  other arithmetic  3.13 us (2%)
    psum x1, waiting for transfers between devices, shards(): down_grad = lax.psum(down_local.astype(jnp.bfloat16), 'replica')[None]  43.6 us
    reduce_scatter x1, waiting for transfers between devices, shards(): lax.psum_scatter(lax.dot_general(inputs, both_back, (((0,), (0,)), ((), (...  20.6 us
    all_gather x1, waiting for transfers between devices, shards(): lax.all_gather(w_gate, 'replica', axis=1, tiled=True)  19.3 us
    all_gather x1, waiting for transfers between devices, shards(): lax.all_gather(w_down, 'replica', axis=2, tiled=True)  12.4 us
    all_to_all x1, starting transfers between devices, shards(): lax.all_to_all(send_weight, 'expert', split_axis=0, concat_axis=0, tiled=...  7.31 us
    all_to_all x1, waiting for transfers between devices, shards(): lax.all_to_all(send_rows, 'expert', split_axis=0, concat_axis=0, tiled=True)  7.13 us
    all_to_all x1, starting transfers between devices, shards(): lax.all_to_all(partial_value.reshape(owners, CAP, width), 'expert', split...  5.52 us
    all_to_all x1, waiting for transfers between devices, shards(): lax.all_to_all(partial_value.reshape(owners, CAP, width), 'expert', split...  5.08 us
  transfers between devices with their start and end apart: 8, of which 7 were waited for; matrix products, arithmetic and copies ran while one was open for 10% of the time, Pallas kernels for 0%

commit v1 on v0

--- a/solution.py
+++ b/solution.py
@@ -97,7 +97,7 @@
     down_local = lax.dot_general(
         hidden, scaled, (((0,), (0,)), ((), ())), preferred_element_type=jnp.float32
     )
-    down_grad = lax.psum(down_local.astype(jnp.bfloat16), "replica")[None]
+    down_grad = jnp.sum(lax.all_gather(down_local.astype(jnp.bfloat16), "replica"), axis=0)[None]
     return (x_grad, gate_grad, up_grad, down_grad)
 
 

time: 172 us -> 178 us (1.035)
  blocking collectives: 0 us -> 12.2 us
  other arithmetic: 3.13 us -> 8.8 us
  starting transfers between devices: 16.4 us -> 10.9 us
  local copies, waits for them, and re-layouts: 9.59 us -> 5.02 us
  waiting for transfers between devices: 115 us -> 113 us
    all_gather x0 -> x1, waiting for transfers between devices: none -> 46.3 us  [shards(): lax.all_gather(down_local.astype(jnp.bfloat16), 'replica')]
    psum x1 -> x0, waiting for transfers between devices: 43.6 us -> none  [shards(): down_grad = lax.psum(down_local.astype(jnp.bfloat16), 'replica')[None]]
    all_to_all x0 -> x1, blocking collectives: none -> 12.2 us  [shards(): lax.all_to_all(partial_value.reshape(owners, CAP, width), 'expert', split...]
    reduce_sum x0 -> x1, other arithmetic: none -> 5.66 us  [shards(): jnp.sum(lax.all_gather(down_local.astype(jnp.bfloat16), 'replica'), axis=0)]
    all_to_all x1 -> x0, starting transfers between devices: 5.52 us -> none  [shards(): lax.all_to_all(partial_value.reshape(owners, CAP, width), 'expert', split...]
    all_to_all x1 -> x0, waiting for transfers between devices: 5.08 us -> none  [shards(): lax.all_to_all(partial_value.reshape(owners, CAP, width), 'expert', split...]
    unnamed x5 -> x4, local copies, waits for them, and re-layouts: 4.58 us -> 0.65 us
  transfers between devices with their start and end apart: 8 -> 7, of which waited for: 7 -> 6; matrix products, arithmetic and copies ran while one was open for 10% -> 9% of each run, Pallas kernels for 0% -> 0%
where the time goes in v1:
time: 178 us; the launch traced here: 177 us
  waiting for transfers between devices  113 us (63%)
  between operations  13.9 us (8%)
  matrix products  13.8 us (8%)
  blocking collectives  12.2 us (7%)
  starting transfers between devices  10.9 us (6%)
  other arithmetic  8.8 us (5%)
  local copies, waits for them, and re-layouts  5.02 us (3%)
    all_gather x1, waiting for transfers between devices, shards(): lax.all_gather(down_local.astype(jnp.bfloat16), 'replica')  46.3 us
    reduce_scatter x1, waiting for transfers between devices, shards(): lax.psum_scatter(lax.dot_general(inputs, both_back, (((0,), (0,)), ((), (...  20.7 us
    all_gather x1, waiting for transfers between devices, shards(): lax.all_gather(w_gate, 'replica', axis=1, tiled=True)  19.3 us
    all_gather x1, waiting for transfers between devices, shards(): lax.all_gather(w_down, 'replica', axis=2, tiled=True)  12.4 us
    all_to_all x1, blocking collectives, shards(): lax.all_to_all(partial_value.reshape(owners, CAP, width), 'expert', split...  12.2 us
    all_to_all x1, starting transfers between devices, shards(): lax.all_to_all(send_weight, 'expert', split_axis=0, concat_axis=0, tiled=...  7.31 us
    all_to_all x1, waiting for transfers between devices, shards(): lax.all_to_all(send_rows, 'expert', split_axis=0, concat_axis=0, tiled=True)  7.13 us
    reduce_sum x1, other arithmetic, shards(): jnp.sum(lax.all_gather(down_local.astype(jnp.bfloat16), 'replica'), axis=0)  5.66 us
  transfers between devices with their start and end apart: 7, of which 6 were waited for; matrix products, arithmetic and copies ran while one was open for 9% of the time, Pallas kernels for 0%

profile of v1, /device:TPU:0, one launch (start us, length us, event | category | flops | bytes accessed | tf_op | source)
XLA Modules:
  0.0 177.5 jit_solution(16903601143496379427)
XLA Ops:
  7.9 0.7 all-gather.6.cloned.1.call-update
  10.0 0.7 convert_reduce_fusion.1
  11.1 0.8 select_reduce_fusion.2
  13.0 0.7 copy.30
  13.7 7.3 %all-to-all-start = ((bf16[8,1,2]{2,1,0:T(2,128)(2,1)}), bf16[8,1,2]{2,1,0:T(2,128)(2,1)S(1)}, u32[]{:S(2)}, u32[]{:S(2)}) async-start(bf16[8,1,2]{2,1,0:T(2,128)(2,1)} %copy.30), calls=%async_computation | async-start | bytes 8192 | tf_op jit(solution)/shard_map/all_to_all | solution.py:36
  21.0 1.4 convolution_convert_fusion
  22.6 4.9 %all-to-all-done = bf16[8,1,2]{2,1,0:T(2,128)(2,1)S(1)} async-done(((bf16[8,1,2]{2,1,0:T(2,128)(2,1)}), bf16[8,1,2]{2,1,0:T(2,128)(2,1)S(1)}, u32[]{:S(2)}, u32[]{:S(2)}) %all-to-all-start) | async-done | bytes 64 | tf_op jit(solution)/shard_map/all_to_all | solution.py:36
  27.5 0.7 broadcast_in_dim.47
  28.2 3.4 %all-to-all-start.1 = ((bf16[8,2,4096]{2,1,0:T(2,128)(2,1)}), bf16[8,2,4096]{2,1,0:T(2,128)(2,1)S(1)}, u32[]{:S(2)}, u32[]{:S(2)}) async-start(bf16[8,2,4096]{2,1,0:T(2,128)(2,1)} %bitcast), calls=%async_computation.1 | async-start | bytes 262144 | tf_op jit(solution)/shard_map/all_to_all | solution.py:35
  31.7 7.1 %all-to-all-done.1 = bf16[8,2,4096]{2,1,0:T(2,128)(2,1)S(1)} async-done(((bf16[8,2,4096]{2,1,0:T(2,128)(2,1)}), bf16[8,2,4096]{2,1,0:T(2,128)(2,1)S(1)}, u32[]{:S(2)}, u32[]{:S(2)}) %all-to-all-start.1) | async-done | bytes 131104 | tf_op jit(solution)/shard_map/all_to_all | solution.py:35
  38.9 1.8 %fusion.16 = f32[16,384]{1,0:T(8,128)S(1)} fusion(bf16[16,4096]{1,0:T(8,128)(2,1)S(1)} %reshape.48, bf16[1,2048,384]{2,1,0:T(8,128)(2,1)} %all-gather.8.cloned.1.call-done), kind=kOutput, calls=%fused_computation.21 | convolution fusion | flops 25165824 | bytes 1662976 | tf_op jit(solution)/shard_map/dot_general | solution.py:52
  40.7 12.4 %all-gather.6.cloned.1.call-done = bf16[1,384,2048]{2,1,0:T(8,128)(2,1)} async-done(((bf16[1,384,512]{2,1,0:T(8,128)(2,1)}), bf16[1,384,2048]{2,1,0:T(8,128)(2,1)}) %all-gather.6.cloned.1.call-update) | async-done | bytes 1572880 | tf_op jit(solution)/shard_map/all_gather | solution.py:41
  53.1 1.9 %fusion.8 = f32[16,384]{1,0:T(8,128)S(1)} fusion(bf16[1,384,2048]{2,1,0:T(8,128)(2,1)} %all-gather.6.cloned.1.call-done, bf16[16,4096]{1,0:T(8,128)(2,1)S(1)} %reshape.48, f32[16]{0:T(128)S(1)} %reshape.51), kind=kOutput, calls=%fused_computation.10 | convolution fusion | flops 25264128 | bytes 1663488 | tf_op jit(solution)/shard_map/dot_general | solution.py:57
  55.1 19.3 %all-gather.10.cloned.1.call-done = bf16[1,2048,384]{2,1,0:T(8,128)(2,1)} async-done(((bf16[1,512,384]{2,1,0:T(8,128)(2,1)}), bf16[1,2048,384]{2,1,0:T(8,128)(2,1)}) %all-gather.10.cloned.1.call-update) | async-done | bytes 1572880 | tf_op jit(solution)/shard_map/all_gather | solution.py:39
  74.4 1.7 multiply_convert_fusion.3
  76.1 2.7 %convolution_convert_fusion.1 = bf16[2048,768]{1,0:T(8,128)(2,1)} fusion(bf16[16,4096]{1,0:T(8,128)(2,1)S(1)} %reshape.48, bf16[16,384]{1,0:T(8,128)(2,1)S(1)} %get-tuple-element.11, bf16[16,384]{1,0:T(8,128)(2,1)S(1)} %get-tuple-element.10), kind=kOutput, calls=%fused_computation.1 | convolution fusion | flops 51953664 | bytes 3235840 | tf_op jit(solution)/shard_map/dot_general | solution.py:85
  79.0 1.8 convolution_convert_fusion.2
  81.4 0.9 fusion.5
  82.4 12.2 %all_to_all.19 = bf16[8,2,2048]{2,1,0:T(2,128)(2,1)S(1)} all-to-all(bf16[8,2,2048]{2,1,0:T(2,128)(2,1)S(1)} %reshape.49), channel_id=1, replica_groups=mesh['expert'=8,'replica'=4] {'expert'}, dimensions={0} | all-to-all | bytes 131072 | tf_op jit(solution)/shard_map/all_to_all | solution.py:67
  95.0 1.1 fusion.4
  96.2 20.7 %reduce-scatter.2.cloned.1.call-done = bf16[512,768]{1,0:T(8,128)(2,1)} async-done(((bf16[2048,768]{1,0:T(8,128)(2,1)}), bf16[512,768]{1,0:T(8,128)(2,1)}) %reduce-scatter.2.cloned.1.call-update) | async-done | bytes 786448 | tf_op jit(solution)/shard_map/reduce_scatter | solution.py:84
  116.9 2.1 %slice_bitcast_fusion = (bf16[1,512,384]{2,1,0:T(8,128)(2,1)}, bf16[1,512,384]{2,1,0:T(8,128)(2,1)}) fusion(bf16[512,768]{1,0:T(8,128)(2,1)} %reduce-scatter.2.cloned.1.call-done), kind=kLoop, calls=%fused_computation.15 | loop fusion | bytes 1572864 | tf_op jit(solution)/shard_map/broadcast_in_dim | solution.py:96
  119.0 46.3 %all-gather.12.cloned.1.call-done = bf16[1536,2048]{1,0:T(8,128)(2,1)} async-done(((bf16[384,2048]{1,0:T(8,128)(2,1)}), bf16[1536,2048]{1,0:T(8,128)(2,1)}) %all-gather.12.cloned.1.call-update) | async-done | bytes 6291472 | tf_op jit(solution)/shard_map/all_gather | solution.py:100
  165.3 5.7 %reduce_sum.52 = bf16[384,2048]{1,0:T(8,128)(2,1)} reduce(bf16[4,384,2048]{2,1,0:T(8,128)(2,1)} %bitcast.26, bf16[]{:T(256)} %constant.20.clone.1), dimensions={0}, to_apply=%region_7.8 | reduce | flops 2359296 | bytes 7864322 | tf_op jit(solution)/shard_map/reduce_sum | solution.py:100
  (34 shorter events, 5.2 us)
Async XLA Ops:
  7.2 31.8 %all-gather.8.cloned.1.call-start = ((), (), s32[]{:S(2)}) async-start(), calls=%async_computation.5 | async-start | bytes 1966080 | tf_op jit(solution)/shard_map/all_gather | solution.py:40
  7.9 45.2 %all-gather.6.cloned.1.call-start = ((), (), s32[]{:S(2)}) async-start(), calls=%async_computation.4 | async-start | bytes 1966080 | tf_op jit(solution)/shard_map/all_gather | solution.py:41
  8.6 65.7 %all-gather.10.cloned.1.call-start = ((), (), s32[]{:S(2)}) async-start(), calls=%async_computation.6 | async-start | bytes 1966080 | tf_op jit(solution)/shard_map/all_gather | solution.py:39
  13.7 13.7 %all-to-all-start = ((bf16[8,1,2]{2,1,0:T(2,128)(2,1)}), bf16[8,1,2]{2,1,0:T(2,128)(2,1)S(1)}, u32[]{:S(2)}, u32[]{:S(2)}) async-start(bf16[8,1,2]{2,1,0:T(2,128)(2,1)} %copy.30), calls=%async_computation | async-start | bytes 8192 | tf_op jit(solution)/shard_map/all_to_all | solution.py:36
  28.2 10.7 %all-to-all-start.1 = ((bf16[8,2,4096]{2,1,0:T(2,128)(2,1)}), bf16[8,2,4096]{2,1,0:T(2,128)(2,1)S(1)}, u32[]{:S(2)}, u32[]{:S(2)}) async-start(bf16[8,2,4096]{2,1,0:T(2,128)(2,1)} %bitcast), calls=%async_computation.1 | async-start | bytes 262144 | tf_op jit(solution)/shard_map/all_to_all | solution.py:35
  31.6 85.4 %reduce-scatter.2.cloned.1.call-start = ((), (), s32[]{:S(2)}) async-start(), calls=%async_computation.7 | async-start | bytes 3932160 | tf_op jit(solution)/shard_map/reduce_scatter | solution.py:84
  78.9 86.4 %all-gather.12.cloned.1.call-start = ((), (), s32[]{:S(2)}) async-start(), calls=%async_computation.8 | async-start | bytes 7864320 | tf_op jit(solution)/shard_map/all_gather | solution.py:100
  78.9 1.8 %copy-start = (bf16[1,2048,384]{2,1,0:T(8,128)(2,1)S(1)}, bf16[1,2048,384]{2,1,0:T(8,128)(2,1)}, u32[]{:S(2)}) copy-start(bf16[1,2048,384]{2,1,0:T(8,128)(2,1)} %all-gather.8.cloned.1.call-done) | copy-start | bytes 4718596
  78.9 2.4 %copy-start.1 = (bf16[1,2048,384]{2,1,0:T(8,128)(2,1)S(1)}, bf16[1,2048,384]{2,1,0:T(8,128)(2,1)}, u32[]{:S(2)}) copy-start(bf16[1,2048,384]{2,1,0:T(8,128)(2,1)} %all-gather.10.cloned.1.call-done) | copy-start | bytes 4718596
Sparse Core Ops, SparseCore 0:
  9.5 22.3 all-gather.7
  33.5 19.6 all-gather.5
  54.7 19.6 all-gather.9
  79.0 37.8 reduce-scatter.1
  118.9 46.3 all-gather.11
